TPU v7x, 32 devices: a whole 2x2x4 slice. The times are simulated.
32 devices in a mesh: dp: 16 (over z, x, core), mp: 2 (over y).
Axes of the slice: x: 2, y: 2, z: 4, core: 2. Of those that a mesh axis runs over, the one named last changes fastest.
Arguments:
- features: bfloat16 [2048, 512], P('dp'), may hold values from -6 to 6
- w_in: bfloat16 [512, 512], P(None, 'mp'), may hold values from -0.25 to 0.25
- b_in: float32 [512], P('mp'), may hold values from -1 to 1
- w_out: bfloat16 [512, 128], P('mp'), may hold values from -0.25 to 0.25
- partner: int32 [2048], P('dp'), may hold values from 0 to 2047, as said below
- window: int32 [16], replicated, may hold values from 0 to 3
Outputs:
- row_loss: float32 [512], P('dp')
- grad_w_in: float32 [512, 512], P(None, 'mp')
- grad_b_in: float32 [512], P('mp')
- grad_w_out: float32 [512, 128], P('mp')
Inputs may be any that keep to these rules, and one draw needn't show every extreme that they name: partner pairs the rows: partner[partner[i]] = i and partner[i] != i for every row i.
All inputs are finite; a program needn't handle non-finite values.
Results may differ from a plain program's by a relative error of at most 0.0027.
Values may be sent and summed in bfloat16 or wider, within the bound.
A program may use at most 64 MiB of HBM per device.

v0:
```python
import math
import jax
import jax.numpy as jnp
from jax import lax
from jax.sharding import PartitionSpec as P

A_DEV = 32
INV_TEMP = 10.0
SHIFT = 10.0
EPS = 1e-06


def contract_rows(left, right):
    return lax.dot_general(
        left, right, (((0,), (0,)), ((), ())), preferred_element_type=jnp.float32
    )


def on_device(features, w_in, b_in, w_out, partner, window):
    rows = features.shape[0]
    parts = lax.axis_size("mp")
    part = lax.axis_index("mp")
    shards = lax.axis_size("dp")
    shard = lax.axis_index("dp")
    width = rows // parts
    anchor_rows = A_DEV
    anchor_all = anchor_rows * shards
    pre = jnp.dot(features, w_in, preferred_element_type=jnp.float32) + b_in
    hidden = jax.nn.silu(pre).astype(jnp.bfloat16)
    proj = lax.psum(jnp.dot(hidden, w_out, preferred_element_type=jnp.float32), "mp")
    norm = jnp.sqrt(jnp.sum(proj * proj, axis=1, keepdims=True) + EPS)
    emb = (proj / norm).astype(jnp.bfloat16)
    embed = emb.shape[1]
    own_cols = lax.dynamic_slice_in_dim(emb, part * width, width, 0)
    columns = lax.all_gather(own_cols, "dp", axis=0, tiled=True)
    col_total = columns.shape[0]
    shard_ids = jnp.arange(shards, dtype=jnp.int32)
    my_block = jnp.sum(jnp.where(shard_ids == shard, window, 0))
    my_start = my_block * anchor_rows
    anchors = lax.dynamic_slice_in_dim(emb, my_start, anchor_rows, 0)
    anchor_partner = lax.dynamic_slice_in_dim(partner, my_start, anchor_rows, 0)
    anchor_ids = shard * rows + my_start + jnp.arange(anchor_rows, dtype=jnp.int32)

    def column_ids(start, count):
        local = start + jnp.arange(count, dtype=jnp.int32)
        return local // width * rows + part * width + local % width

    blk = math.gcd(col_total, 2048)
    nblk = col_total // blk
    col_blocks = columns.reshape(nblk, blk, embed)
    starts = jnp.arange(nblk, dtype=jnp.int32) * blk

    def forward(carry, item):
        total, hit = carry
        block, start = item
        s = jnp.dot(anchors, block.T, preferred_element_type=jnp.float32) * INV_TEMP
        ids = column_ids(start, blk)
        ex = jnp.where(ids[None, :] == anchor_ids[:, None], 0.0, jnp.exp(s - SHIFT))
        hit = hit + jnp.sum(jnp.where(ids[None, :] == anchor_partner[:, None], s, 0.0), axis=1)
        return ((total + jnp.sum(ex, axis=1), hit), None)

    zero_rows = jnp.zeros((anchor_rows,), jnp.float32)
    (total, hit), _ = lax.scan(forward, (zero_rows, zero_rows), (col_blocks, starts))
    total, hit = lax.psum((total, hit), "mp")
    row_loss = jnp.log(total) + SHIFT - hit

    def row_weights(s, ids):
        prob = jnp.where(
            ids[None, :] == anchor_ids[:, None], 0.0, jnp.exp(s - SHIFT) / total[:, None]
        )
        onehot = (ids[None, :] == anchor_partner[:, None]).astype(jnp.float32)
        return (prob - onehot).astype(jnp.bfloat16)

    def backward(acc, item):
        block, start = item
        s = jnp.dot(anchors, block.T, preferred_element_type=jnp.float32) * INV_TEMP
        weights = row_weights(s, column_ids(start, blk))
        return (acc + jnp.dot(weights, block, preferred_element_type=jnp.float32), None)

    row_part, _ = lax.scan(
        backward, jnp.zeros((anchor_rows, embed), jnp.float32), (col_blocks, starts)
    )
    totals = lax.all_gather(total, "dp", axis=0, tiled=True)
    own_ids = shard * rows + part * width + jnp.arange(width, dtype=jnp.int32)
    own_partner = lax.dynamic_slice_in_dim(partner, part * width, width, 0)
    piece = lax.all_gather(anchors, "dp", axis=0, tiled=True)
    count = piece.shape[0]
    inner = math.gcd(count, 2048)
    sub_pieces = piece.reshape(count // inner, inner, embed)
    offsets = jnp.arange(count // inner, dtype=jnp.int32) * inner

    def one_block(inner_acc, item):
        block, offset = item
        block_totals = lax.dynamic_slice_in_dim(totals, offset, inner, 0)
        flat = offset + jnp.arange(inner, dtype=jnp.int32)
        owner = flat // anchor_rows
        owner_block = jnp.sum(
            jnp.where(owner[:, None] == shard_ids[None, :], window[None, :], 0), axis=1
        )
        ids = owner * rows + owner_block * anchor_rows + flat % anchor_rows
        s = jnp.dot(own_cols, block.T, preferred_element_type=jnp.float32) * INV_TEMP
        prob = jnp.where(
            ids[None, :] == own_ids[:, None], 0.0, jnp.exp(s - SHIFT) / block_totals[None, :]
        )
        onehot = (ids[None, :] == own_partner[:, None]).astype(jnp.float32)
        weights = (prob - onehot).astype(jnp.bfloat16)
        return (inner_acc + jnp.dot(weights, block, preferred_element_type=jnp.float32), None)

    result, _ = lax.scan(one_block, jnp.zeros((width, embed), jnp.float32), (sub_pieces, offsets))
    placed = lax.dynamic_update_slice_in_dim(
        jnp.zeros((rows, embed), jnp.float32), result, part * width, 0
    )
    row_placed = lax.dynamic_update_slice_in_dim(
        jnp.zeros((rows, embed), jnp.float32), row_part, my_start, 0
    )
    grad_emb = lax.psum(row_placed + placed, "mp") * (INV_TEMP / anchor_all)
    unit = proj / norm
    grad_proj = ((grad_emb - unit * jnp.sum(unit * grad_emb, axis=1, keepdims=True)) / norm).astype(
        jnp.bfloat16
    )
    grad_w_out = contract_rows(hidden, grad_proj)
    grad_hidden = lax.dot_general(
        grad_proj, w_out, (((1,), (1,)), ((), ())), preferred_element_type=jnp.float32
    )
    sig = jax.nn.sigmoid(pre)
    grad_pre = (grad_hidden * sig * (1.0 + pre * (1.0 - sig))).astype(jnp.bfloat16)
    grad_w_in = contract_rows(features, grad_pre)
    grad_b_in = jnp.sum(grad_pre.astype(jnp.float32), axis=0)
    grad_w_in, grad_b_in, grad_w_out = lax.psum((grad_w_in, grad_b_in, grad_w_out), "dp")
    return (row_loss, grad_w_in, grad_b_in, grad_w_out)


def solution(mesh):
    return jax.shard_map(
        on_device,
        mesh=mesh,
        in_specs=(P("dp", None), P(None, "mp"), P("mp"), P("mp", None), P("dp"), P()),
        out_specs=(P("dp"), P(None, "mp"), P("mp"), P("mp", None)),
        check_vma=False,
    )
```

profile of v0, /device:TPU:0, one launch (start us, length us, event | category | flops | bytes accessed | tf_op | source)
XLA Modules:
  0.0 234.8 jit_solution(11536599049466594532)
XLA Ops:
  7.2 0.9 copy-done
  8.1 1.1 multiply_convert_fusion
  9.3 0.8 fusion.57
  10.1 0.6 copy-done.7
  10.8 0.6 fusion.50
  12.1 0.6 copy-done.8
  13.0 0.6 copy-done.9
  13.7 0.6 dynamic-slice.3
  14.9 19.6 %all-reduce.7.cloned.1.call-done = f32[128,128]{1,0:T(8,128)} async-done(((f32[128,128]{1,0:T(8,128)}), f32[128,128]{1,0:T(8,128)}) %all-reduce.7.cloned.1.call-update) | async-done | bytes 65552 | tf_op jit(solution)/shard_map/psum | solution.py:30
  34.5 1.0 multiply_reduce_fusion.1
  35.7 21.7 %all_gather.10 = bf16[512,128]{1,0:T(8,128)(2,1)S(1)} all-gather(bf16[32,128]{1,0:T(8,128)(2,1)S(1)} %constant_dynamic-slice_fusion.1), channel_id=1, replica_groups=mesh['dp'=16,'mp'=2] {'dp'}, dimensions={0}, use_global_device_ids=true | all-gather | bytes 139264 | tf_op jit(solution)/shard_map/all_gather | solution.py:86
  57.4 18.1 %all_gather.9 = bf16[1024,128]{1,0:T(8,128)(2,1)S(1)} all-gather(bf16[64,128]{1,0:T(8,128)(2,1)S(1)} %constant_dynamic-slice_fusion), channel_id=1, replica_groups=mesh['dp'=16,'mp'=2] {'dp'}, dimensions={0}, use_global_device_ids=true | all-gather | bytes 278528 | tf_op jit(solution)/shard_map/all_gather | solution.py:35
  75.8 4.9 %all-reduce.2 = (f32[32]{0:T(128)S(1)}, f32[32]{0:T(128)S(1)}) all-reduce(f32[32]{0:T(128)S(1)} %get-tuple-element.70, f32[32]{0:T(128)S(1)} %get-tuple-element.69), channel_id=1, replica_groups=mesh['dp'=16,'mp'=2] {'mp'}, use_global_device_ids=true, to_apply=%region_6.7 | all-reduce | flops 64 | bytes 512 | tf_op jit(solution)/shard_map/psum | solution.py:64
  81.0 29.9 %all-reduce = f32[512]{0:T(512)S(1)} all-reduce(f32[512]{0:T(512)S(1)} %dynamic-update-slice.1), channel_id=1, replica_groups=mesh['dp'=16,'mp'=2] {'dp'}, use_global_device_ids=true, to_apply=%add | all-reduce | flops 512 | bytes 4096
  111.5 0.6 copy-done.3
  112.2 17.4 %all-reduce.9.cloned.1.call-done = f32[128,128]{1,0:T(8,128)} async-done(((f32[128,128]{1,0:T(8,128)}), f32[128,128]{1,0:T(8,128)}) %all-reduce.9.cloned.1.call-update) | async-done | bytes 65552 | tf_op jit(solution)/shard_map/psum | solution.py:116
  129.6 1.1 multiply_reduce_fusion
  130.8 0.9 fusion.58
  131.8 0.7 copy-done.5
  132.5 1.0 convolution_bitcast_fusion
  134.1 33.6 %psum.54 = f32[256]{0:T(256)} all-reduce(f32[256]{0:T(256)S(1)} %get-tuple-element.87), channel_id=1, replica_groups=mesh['dp'=16,'mp'=2] {'dp'}, use_global_device_ids=true, to_apply=%region_12.13 | all-reduce | flops 256 | bytes 2048 | tf_op jit(solution)/shard_map/psum | solution.py:129
  167.7 57.9 %all-reduce.11.cloned.1.call-done = (f32[512,256]{0,1:T(8,128)}, f32[256,128]{1,0:T(8,128)}) async-done(((f32[512,256]{0,1:T(8,128)}, f32[256,128]{1,0:T(8,128)}), (f32[512,256]{0,1:T(8,128)}, f32[256,128]{1,0:T(8,128)})) %all-reduce.11.cloned.1.call-update) | async-done | bytes 655376 | tf_op jit(solution)/shard_map/psum | solution.py:129
  225.5 2.1 copy.11
  227.6 0.7 copy.19
  (41 shorter events, 2.5 us)
Async XLA Ops:
  7.2 1.0 copy-start
  7.2 2.1 copy-start.6
  7.2 27.3 %all-reduce.7.cloned.1.call-start = ((), (), s32[]{:S(2)}) async-start(), calls=%async_computation | async-start | bytes 131072 | tf_op jit(solution)/shard_map/psum | solution.py:30
  10.1 119.5 %all-reduce.9.cloned.1.call-start = ((), (), s32[]{:S(2)}) async-start(), calls=%async_computation.1 | async-start | bytes 131072 | tf_op jit(solution)/shard_map/psum | solution.py:116
  10.1 0.7 copy-start.7
  12.1 0.7 copy-start.8
  13.0 0.7 copy-start.9
  34.5 1.0 copy-start.1
  111.4 0.6 copy-start.3
  112.1 113.4 %all-reduce.11.cloned.1.call-start = ((), (), s32[]{:S(2)}) async-start(), calls=%async_computation.2 | async-start | bytes 1310720 | tf_op jit(solution)/shard_map/psum | solution.py:129
  129.6 1.1 copy-start.2
  131.6 0.9 copy-start.5
  225.5 2.1 copy-start.4
Sparse Core Ops, SparseCore 0:
  10.8 23.6 all-reduce.6
  112.2 17.2 all-reduce.8
  133.7 91.7 all-reduce.10
where the time goes:
time: 235 us
  blocking collectives  108 us (46%)
  waiting for transfers between devices  94.9 us (40%)
  between operations  15.3 us (7%)
  local copies, waits for them, and re-layouts  7.86 us (3%)
  matrix products  4.84 us (2%)
  other arithmetic  3.56 us (2%)
    psum x1, waiting for transfers between devices, on_device(): lax.psum((grad_w_in, grad_b_in, grad_w_out), 'dp')  57.9 us
    psum x1, blocking collectives, on_device(): lax.psum((grad_w_in, grad_b_in, grad_w_out), 'dp')  33.6 us
    unnamed x1, blocking collectives  29.9 us
    all_gather x1, blocking collectives, on_device(): piece = lax.all_gather(anchors, 'dp', axis=0, tiled=True)  21.7 us
    psum x1, waiting for transfers between devices, on_device(): lax.psum(jnp.dot(hidden, w_out, preferred_element_type=jnp.float32), 'mp')  19.6 us
    all_gather x1, blocking collectives, on_device(): columns = lax.all_gather(own_cols, 'dp', axis=0, tiled=True)  18.1 us
    psum x1, waiting for transfers between devices, on_device(): grad_emb = lax.psum(row_placed + placed, 'mp') * (INV_TEMP / anchor_all)  17.4 us
    unnamed x25, local copies, waits for them, and re-layouts  7.68 us
  transfers between devices with their start and end apart: 3, of which 3 were waited for; matrix products, arithmetic and copies ran while one was open for 1% of the time, Pallas kernels for 0%

commit v1 on v0

--- a/solution.py
+++ b/solution.py
@@ -113,7 +113,12 @@
     row_placed = lax.dynamic_update_slice_in_dim(
         jnp.zeros((rows, embed), jnp.float32), row_part, my_start, 0
     )
-    grad_emb = lax.psum(row_placed + placed, "mp") * (INV_TEMP / anchor_all)
+
+    def mix_the_roots(array_in):
+        r_now = lax.all_gather(array_in, "mp")
+        return jnp.sum(r_now, axis=0)
+
+    grad_emb = mix_the_roots(row_placed + placed) * (INV_TEMP / anchor_all)
     unit = proj / norm
     grad_proj = ((grad_emb - unit * jnp.sum(unit * grad_emb, axis=1, keepdims=True)) / norm).astype(
         jnp.bfloat16

time: 235 us -> 218 us (0.928)
  waiting for transfers between devices: 94.9 us -> 77.2 us
    psum x1 -> x0, waiting for transfers between devices: 17.4 us -> none  [on_device(): grad_emb = lax.psum(row_placed + placed, 'mp') * (INV_TEMP / anchor_all)]
    all_gather x0 -> x1, blocking collectives: none -> 4.93 us  [mix_the_roots(): r_now = lax.all_gather(array_in, 'mp')]
    psum x1, blocking collectives: 33.6 us -> 30.2 us  [on_device(): lax.psum((grad_w_in, grad_b_in, grad_w_out), 'dp')]
    unnamed x25 -> x22, local copies, waits for them, and re-layouts: 7.68 us -> 7.06 us
  transfers between devices with their start and end apart: 3 -> 2, of which waited for: 3 -> 2; matrix products, arithmetic and copies ran while one was open for 1% -> 1% of each run, Pallas kernels for 0% -> 0%
where the time goes in v1:
time: 218 us; the launch traced here: 217 us
  blocking collectives  110 us (50%)
  waiting for transfers between devices  77.2 us (35%)
  between operations  15.5 us (7%)
  local copies, waits for them, and re-layouts  7.23 us (3%)
  matrix products  4.86 us (2%)
  other arithmetic  2.68 us (1%)
    psum x1, waiting for transfers between devices, on_device(): lax.psum((grad_w_in, grad_b_in, grad_w_out), 'dp')  57.6 us
    psum x1, blocking collectives, on_device(): lax.psum((grad_w_in, grad_b_in, grad_w_out), 'dp')  30.2 us
    unnamed x1, blocking collectives  29.9 us
    all_gather x1, blocking collectives, on_device(): piece = lax.all_gather(anchors, 'dp', axis=0, tiled=True)  21.7 us
    psum x1, waiting for transfers between devices, on_device(): lax.psum(jnp.dot(hidden, w_out, preferred_element_type=jnp.float32), 'mp')  19.6 us
    all_gather x1, blocking collectives, on_device(): columns = lax.all_gather(own_cols, 'dp', axis=0, tiled=True)  18.1 us
    unnamed x22, local copies, waits for them, and re-layouts  7.06 us
    all_gather x1, blocking collectives, mix_the_roots(): r_now = lax.all_gather(array_in, 'mp')  4.93 us
  transfers between devices with their start and end apart: 2, of which 2 were waited for; matrix products, arithmetic and copies ran while one was open for 1% of the time, Pallas kernels for 0%

profile of v1, /device:TPU:0, one launch (start us, length us, event | category | flops | bytes accessed | tf_op | source)
XLA Modules:
  0.0 217.4 jit_solution(14637820728655598038)
XLA Ops:
  7.2 0.9 copy-done
  8.1 1.1 multiply_convert_fusion
  9.3 0.8 fusion.58
  10.1 0.6 copy-done.5
  10.8 0.6 fusion.51
  12.1 0.6 copy-done.6
  13.0 0.6 copy-done.7
  13.7 0.6 dynamic-slice.3
  14.9 19.6 %all-reduce.6.cloned.1.call-done = f32[128,128]{1,0:T(8,128)} async-done(((f32[128,128]{1,0:T(8,128)}), f32[128,128]{1,0:T(8,128)}) %all-reduce.6.cloned.1.call-update) | async-done | bytes 65552 | tf_op jit(solution)/shard_map/psum | solution.py:30
  34.5 1.0 multiply_reduce_fusion.1
  35.7 21.7 %all_gather.19 = bf16[512,128]{1,0:T(8,128)(2,1)S(1)} all-gather(bf16[32,128]{1,0:T(8,128)(2,1)S(1)} %constant_dynamic-slice_fusion.1), channel_id=1, replica_groups=mesh['dp'=16,'mp'=2] {'dp'}, dimensions={0}, use_global_device_ids=true | all-gather | bytes 139264 | tf_op jit(solution)/shard_map/all_gather | solution.py:86
  57.4 18.1 %all_gather.17 = bf16[1024,128]{1,0:T(8,128)(2,1)S(1)} all-gather(bf16[64,128]{1,0:T(8,128)(2,1)S(1)} %constant_dynamic-slice_fusion), channel_id=1, replica_groups=mesh['dp'=16,'mp'=2] {'dp'}, dimensions={0}, use_global_device_ids=true | all-gather | bytes 278528 | tf_op jit(solution)/shard_map/all_gather | solution.py:35
  75.8 4.9 %all-reduce.2 = (f32[32]{0:T(128)S(1)}, f32[32]{0:T(128)S(1)}) all-reduce(f32[32]{0:T(128)S(1)} %get-tuple-element.83, f32[32]{0:T(128)S(1)} %get-tuple-element.82), channel_id=1, replica_groups=mesh['dp'=16,'mp'=2] {'mp'}, use_global_device_ids=true, to_apply=%region_6.7 | all-reduce | flops 64 | bytes 512 | tf_op jit(solution)/shard_map/psum | solution.py:64
  81.0 29.9 %all-reduce = f32[512]{0:T(512)S(1)} all-reduce(f32[512]{0:T(512)S(1)} %dynamic-update-slice.2), channel_id=1, replica_groups=mesh['dp'=16,'mp'=2] {'dp'}, use_global_device_ids=true, to_apply=%add | all-reduce | flops 512 | bytes 4096
  111.1 0.3 fusion.11
  111.5 4.9 %all_gather.22 = f32[2,128,128]{2,1,0:T(8,128)S(1)} all-gather(f32[1,128,128]{2,1,0:T(8,128)S(1)} %fusion.11), channel_id=1, replica_groups=mesh['dp'=16,'mp'=2] {'mp'}, dimensions={0}, use_global_device_ids=true | all-gather | bytes 196608 | tf_op jit(solution)/shard_map/all_gather | solution.py:118
  116.7 0.9 fusion.59
  117.8 0.7 copy-done.3
  118.5 1.0 convolution_bitcast_fusion
  119.5 30.2 %psum.46 = f32[256]{0:T(256)} all-reduce(f32[256]{0:T(256)S(1)} %get-tuple-element.100), channel_id=1, replica_groups=mesh['dp'=16,'mp'=2] {'dp'}, use_global_device_ids=true, to_apply=%region_12.13 | all-reduce | flops 256 | bytes 2048 | tf_op jit(solution)/shard_map/psum | solution.py:134
  149.7 0.5 add_subtract_fusion
  150.3 57.6 %all-reduce.8.cloned.1.call-done = (f32[512,256]{0,1:T(8,128)}, f32[256,128]{1,0:T(8,128)}) async-done(((f32[512,256]{0,1:T(8,128)}, f32[256,128]{1,0:T(8,128)}), (f32[512,256]{0,1:T(8,128)}, f32[256,128]{1,0:T(8,128)})) %all-reduce.8.cloned.1.call-update) | async-done | bytes 655376 | tf_op jit(solution)/shard_map/psum | solution.py:134
  207.9 2.1 copy.12
  209.9 0.7 copy.19
  (37 shorter events, 1.8 us)
Async XLA Ops:
  7.2 1.0 copy-start
  7.2 2.1 copy-start.4
  7.2 27.3 %all-reduce.6.cloned.1.call-start = ((), (), s32[]{:S(2)}) async-start(), calls=%async_computation | async-start | bytes 131072 | tf_op jit(solution)/shard_map/psum | solution.py:30
  10.1 197.8 %all-reduce.8.cloned.1.call-start = ((), (), s32[]{:S(2)}) async-start(), calls=%async_computation.1 | async-start | bytes 1310720 | tf_op jit(solution)/shard_map/psum | solution.py:134
  10.1 0.7 copy-start.5
  12.1 0.7 copy-start.6
  13.0 0.7 copy-start.7
  34.5 1.0 copy-start.1
  117.6 0.9 copy-start.3
  207.9 2.1 copy-start.2
Sparse Core Ops, SparseCore 0:
  10.8 23.6 all-reduce.5
  119.7 88.1 all-reduce.7
